TPU v7x, 128 devices: a whole 4x4x4 slice. The times are simulated.
128 devices in a mesh: dp: 4 (over y), row: 8 (over x, core), col: 4 (over z).
Axes of the slice: x: 4, y: 4, z: 4, core: 2. Of those that a mesh axis runs over, the one named last changes fastest.
Arguments:
- patches: bfloat16 [8, 128, 128, 768], P('dp', 'row', 'col'), may hold values from -64 to 64
- keep_mask: int32 [8, 128, 128], P('dp', 'row', 'col'), may hold values from 0 to 1, as said below
- mask_token: bfloat16 [768], replicated, may hold values from -6 to 6
- qkv_weight: bfloat16 [768, 2304], replicated, may hold values from -2 to 2
- out_weight: bfloat16 [768, 768], replicated, may hold values from -0.21875 to 0.21875
- up_weight: bfloat16 [768, 3072], P(None, 'dp'), may hold values from -0.21875 to 0.21875
- down_weight: bfloat16 [3072, 768], P('dp'), may hold values from -0.109375 to 0.109375
- dec_proj: bfloat16 [768, 256], replicated, may hold values from -0.21875 to 0.21875
- conv_weight: bfloat16 [2, 9, 256, 256], replicated, may hold values from -0.125 to 0.125
- head_weight: bfloat16 [256, 128], replicated, may hold values from -0.375 to 0.375
Outputs:
- recon: bfloat16 [8, 128, 128, 128], P('dp', 'row', 'col')
Inputs may be any that keep to these rules, and one draw needn't show every extreme that they name: `keep_mask`: each sample has exactly 4096 ones; in every sample the 16 x 32 tile of some device is all ones.
All inputs are finite; a program needn't handle non-finite values.
Results may differ from a plain program's by a relative error of at most 0.015.
Values may be sent and summed in bfloat16 or wider, within the bound.
No kernel may reach another device: no remote copies, remote signals or barrier semaphores. Data moves between devices by JAX's collectives and lax.ppermute only.
A program may use at most 192 MiB of HBM per device.

v0:
```python
import jax
import jax.numpy as jnp
from jax import lax
from jax.sharding import PartitionSpec as P

HEADS = 12
HD = 64
EPS = 1e-06
BLOCK = 512


def extended_2(cells, sides, width):
    for axis, dim in sides:
        count = lax.axis_size(axis)
        ends = count - 1
        head = lax.slice_in_dim(cells, 0, width, axis=dim)
        tail = lax.slice_in_dim(cells, cells.shape[dim] - width, cells.shape[dim], axis=dim)
        cells = jnp.concatenate(
            [
                lax.ppermute(tail, axis, [(i, (i + 1) % count) for i in range(ends)]),
                cells,
                lax.ppermute(head, axis, [((i + 1) % count, i) for i in range(ends)]),
            ],
            axis=dim,
        )
    return cells


def normalize(rows):
    wide = rows.astype(jnp.float32)
    mean = jnp.mean(wide, -1, keepdims=True)
    centred = wide - mean
    var = jnp.mean(centred * centred, -1, keepdims=True)
    return (centred * lax.rsqrt(var + EPS)).astype(jnp.bfloat16)


def attend(carry, query, keys, values):
    run_max, run_sum, store = carry
    scores = jnp.einsum("sqhd,skhd->shqk", query, keys, preferred_element_type=jnp.float32) * 0.125
    new_max = jnp.maximum(run_max, jnp.max(scores, -1))
    shrink = jnp.exp(run_max - new_max)
    expo = jnp.exp(scores - new_max[..., None])
    run_sum = run_sum * shrink + jnp.sum(expo, -1)
    added = jnp.einsum(
        "shqk,skhd->sqhd", expo.astype(jnp.bfloat16), values, preferred_element_type=jnp.float32
    )
    store = store * jnp.swapaxes(shrink, 1, 2)[..., None] + added
    return (new_max, run_sum, store)


def convolve(extended, taps, out_h, out_w):
    total = None
    for first in range(3):
        for second in range(3):
            term = jnp.einsum(
                "shwc,cd->shwd",
                extended[:, first : first + out_h, second : second + out_w],
                taps[first * 3 + second],
                preferred_element_type=jnp.float32,
            )
            total = term if total is None else total + term
    return total


def border(field):
    return extended_2(field, (("row", 1), ("col", 2)), 1)


def shards(
    patches,
    keep_mask,
    mask_token,
    qkv_weight,
    out_weight,
    up_weight,
    down_weight,
    dec_proj,
    conv_weight,
    head_weight,
):
    peers = lax.axis_size(("row", "col"))
    me = lax.axis_index(("row", "col"))
    samples, tile_h, tile_w, width = patches.shape
    tile = tile_h * tile_w
    cap = tile // peers
    kept_dev = tile // 4
    flat_tokens = patches.reshape(samples, tile, width)
    flat_mask = keep_mask.reshape(samples, tile)
    counts = jnp.sum(flat_mask, 1)
    every_count = lax.all_gather(counts[None, :], ("row", "col"), axis=0, tiled=True)
    ends = jnp.cumsum(every_count, 0)
    starts = ends - every_count
    my_start = lax.dynamic_index_in_dim(starts, me, 0, keepdims=False)
    running = jnp.cumsum(flat_mask, 1)
    positions = jnp.arange(tile, dtype=jnp.int32)
    kept_at = jnp.sum((running[:, None, :] <= positions[None, :, None]).astype(jnp.int32), 2)
    peer_ids = jnp.arange(peers, dtype=jnp.int32)
    slot_ids = jnp.arange(cap, dtype=jnp.int32)
    sample_ids = jnp.arange(samples, dtype=jnp.int32)[None, :, None]
    local_rank = slot_ids[None, None, :] * peers + jnp.mod(
        peer_ids[:, None, None] - my_start[None, :, None], peers
    )
    live = local_rank < counts[None, :, None]
    source_pos = kept_at[sample_ids, jnp.minimum(local_rank, tile - 1)]
    outgoing = jnp.where(
        live[..., None], flat_tokens[sample_ids, source_pos], jnp.zeros((), jnp.bfloat16)
    )
    arrived = lax.all_to_all(outgoing, ("row", "col"), split_axis=0, concat_axis=0, tiled=True)
    order_rank = jnp.arange(kept_dev, dtype=jnp.int32) * peers + me
    source_of = jnp.sum((ends[:, :, None] <= order_rank[None, None, :]).astype(jnp.int32), 0)
    start_of = jnp.take_along_axis(starts.T, source_of, 1)
    slot_of = (order_rank[None, :] - start_of) // peers
    rows_in = arrived[source_of, jnp.arange(samples, dtype=jnp.int32)[:, None], slot_of]
    flat_rows = rows_in.reshape(samples * kept_dev, width)
    normed = normalize(flat_rows)
    init_carry = (
        jnp.full((samples, HEADS, kept_dev), -1e30, jnp.float32),
        jnp.zeros((samples, HEADS, kept_dev), jnp.float32),
        jnp.zeros((samples, kept_dev, HEADS, HD), jnp.float32),
    )
    qkv = jnp.dot(normed, qkv_weight, preferred_element_type=jnp.float32).astype(jnp.bfloat16)
    query = qkv[:, :width].reshape(samples, kept_dev, HEADS, HD)
    keys_local = qkv[:, width : 2 * width].reshape(samples, kept_dev, width)
    values_local = qkv[:, 2 * width :].reshape(samples, kept_dev, width)
    carry = init_carry
    keys_piece = lax.all_gather(keys_local, ("row", "col"), axis=1, tiled=True)
    values_piece = lax.all_gather(values_local, ("row", "col"), axis=1, tiled=True)
    count = keys_piece.shape[1]
    for lower in range(0, count, BLOCK):
        upper = min(count, lower + BLOCK)
        keys_block = keys_piece[:, lower:upper].reshape(samples, upper - lower, HEADS, HD)
        values_block = values_piece[:, lower:upper].reshape(samples, upper - lower, HEADS, HD)
        carry = attend(carry, query, keys_block, values_block)
    run_max, run_sum, store = carry
    attn = (
        (store / jnp.swapaxes(run_sum, 1, 2)[..., None])
        .astype(jnp.bfloat16)
        .reshape(samples * kept_dev, width)
    )
    x_one = (
        flat_rows.astype(jnp.float32)
        + jnp.dot(attn, out_weight, preferred_element_type=jnp.float32)
    ).astype(jnp.bfloat16)
    normed_two = normalize(x_one)
    hidden = jax.nn.gelu(
        jnp.dot(
            normed_two,
            lax.all_gather(up_weight, "dp", axis=1, tiled=True),
            preferred_element_type=jnp.float32,
        ),
        approximate=False,
    ).astype(jnp.bfloat16)
    feed = jnp.dot(
        hidden,
        lax.all_gather(down_weight, "dp", axis=0, tiled=True),
        preferred_element_type=jnp.float32,
    )
    encoded = (
        (x_one.astype(jnp.float32) + feed).astype(jnp.bfloat16).reshape(samples, kept_dev, width)
    )
    back_rank = slot_ids[None, None, :] * peers + jnp.mod(me - starts[:, :, None], peers)
    back_live = back_rank < every_count[:, :, None]
    back_row = jnp.minimum((starts[:, :, None] + back_rank) // peers, kept_dev - 1)
    returning = jnp.where(
        back_live[..., None], encoded[sample_ids, back_row], jnp.zeros((), jnp.bfloat16)
    )
    home = lax.all_to_all(returning, ("row", "col"), split_axis=0, concat_axis=0, tiled=True)
    kept_rank = jnp.maximum(running - 1, 0)
    target_peer = jnp.mod(my_start[:, None] + kept_rank, peers)
    token_back = home[
        target_peer, jnp.arange(samples, dtype=jnp.int32)[:, None], kept_rank // peers
    ]
    filled = jnp.where(flat_mask[..., None] == 1, token_back, mask_token[None, None, :]).reshape(
        samples, tile_h, tile_w, width
    )
    h_zero = jnp.dot(filled, dec_proj, preferred_element_type=jnp.float32).astype(jnp.bfloat16)
    conv_one = convolve(border(h_zero), conv_weight[0], tile_h, tile_w)
    h_one = (h_zero.astype(jnp.float32) + jax.nn.gelu(conv_one, approximate=False)).astype(
        jnp.bfloat16
    )
    conv_two = convolve(border(h_one), conv_weight[1], tile_h, tile_w)
    h_two = (h_one.astype(jnp.float32) + jax.nn.gelu(conv_two, approximate=False)).astype(
        jnp.bfloat16
    )
    return jnp.dot(h_two, head_weight, preferred_element_type=jnp.float32).astype(jnp.bfloat16)


def solution(mesh):
    return jax.shard_map(
        shards,
        mesh=mesh,
        in_specs=(
            P("dp", "row", "col", None),
            P("dp", "row", "col"),
            P(),
            P(),
            P(),
            P(None, "dp"),
            P("dp", None),
            P(),
            P(),
            P(),
        ),
        out_specs=P("dp", "row", "col", None),
        check_vma=False,
    )
```

profile of v0, /device:TPU:2, one launch (start us, length us, event | category | flops | bytes accessed | tf_op | source)
XLA Modules:
  0.0 474.3 jit_solution(3876837634357682865)
XLA Ops:
  11.7 16.4 %all-reduce = s32[64]{0:T(128)} all-reduce(s32[64]{0:T(128)S(1)} %dynamic-update-slice), channel_id=2, replica_groups=mesh['dp'=4,'row'=8,'col'=4] {'row','col'}, use_global_device_ids=true, to_apply=%add | all-reduce | flops 64 | bytes 512
  34.5 1.9 reduce-window.6
  41.8 9.1 %gather_fusion = s32[1024]{0:T(1024)S(1)} fusion(s32[2,512]{1,0:T(2,128)S(1)} %convert_reduce_fusion, s32[1024]{0:T(1024)S(1)} %reshape.722), kind=kCustom, calls=%fused_computation | custom fusion | bytes 16384 | tf_op jit(solution)/shard_map/gather | solution.py:104
  53.8 29.2 %gather_fusion.1 = bf16[1024,768]{1,0:T(8,128)(2,1)} fusion(bf16[2,512,768]{2,1,0:T(8,128)(2,1)} %bitcast.404, s32[1024]{0:T(1024)S(1)} %reshape.728), kind=kCustom, calls=%fused_computation.1 | custom fusion | bytes 3153920 | tf_op jit(solution)/shard_map/gather | solution.py:106
  83.1 2.8 broadcast_select_fusion
  85.9 6.6 %all-to-all-start = ((bf16[32,2,16,768]{3,2,1,0:T(8,128)(2,1)}), bf16[32,2,16,768]{3,2,1,0:T(8,128)(2,1)}, u32[]{:S(2)}, u32[]{:S(2)}) async-start(bf16[32,2,16,768]{3,2,1,0:T(8,128)(2,1)} %broadcast_select_fusion), calls=%async_computation | async-start | bytes 3145728 | tf_op jit(solution)/shard_map/all_to_all | solution.py:108
  95.9 2.7 gather_fusion.5
  99.3 14.7 %all-to-all-done = bf16[32,2,16,768]{3,2,1,0:T(8,128)(2,1)} async-done(((bf16[32,2,16,768]{3,2,1,0:T(8,128)(2,1)}), bf16[32,2,16,768]{3,2,1,0:T(8,128)(2,1)}, u32[]{:S(2)}, u32[]{:S(2)}) %all-to-all-start) | async-done | bytes 1572896 | tf_op jit(solution)/shard_map/all_to_all | solution.py:108
  114.0 4.2 gather_fusion.2
  120.6 2.1 convolution_convert_fusion
  126.2 61.5 %all-gather.6.cloned.1.call-done = bf16[2,4096,768]{2,1,0:T(8,128)(2,1)} async-done(((bf16[2,128,768]{2,1,0:T(8,128)(2,1)}), bf16[2,4096,768]{2,1,0:T(8,128)(2,1)}) %all-gather.6.cloned.1.call-update) | async-done | bytes 12582928 | tf_op jit(solution)/shard_map/all_gather | solution.py:126
  187.7 9.0 %fusion.404 = (bf16[2,512,768]{2,1,0:T(8,128)(2,1)}, bf16[2,512,768]{2,1,0:T(8,128)(2,1)S(1)}, bf16[2,512,768]{2,1,0:T(8,128)(2,1)}, bf16[2,512,768]{2,1,0:T(8,1...) fusion(bf16[2,4096,768]{2,1,0:T(8,128)(2,1)} %all-gather.6.clon, ...), kind=kLoop, calls=%fused_computation.479 | loop fusion | bytes 25165824 | tf_op jit(solution)/shard_map/slice | solution.py:131
  196.7 2.6 copy.63
  200.9 5.3 %multiply_reduce_fusion.7 = (f32[2,12,128]{2,1,0:T(8,128)S(1)}, f32[2,12,128,512]{3,2,1,0:T(8,128)}) fusion(bf16[2,512,12,64]{1,3,2,0:T(8,128)(2,1)} %bitcast.436, bf16[2,128,12,64]{1,0,3,2:T(2,128)(2,1)S(1)} %reshape.700), kind=kOutput, calls=%fused_computation.21 | convolution fusion | flops 204469248 | bytes 8269824 | tf_op jit(solution)/shard_map/sqhd,skhd->shqk/dot_general | solution.py:39
  206.2 3.6 multiply_reduce_fusion
  209.9 1.7 copy.81
  211.6 3.7 multiply_reduce_fusion.1
  215.3 1.7 copy.78
  217.0 3.7 multiply_reduce_fusion.2
  220.8 1.7 copy.75
  222.5 3.7 multiply_reduce_fusion.3
  226.2 1.7 copy.72
  227.9 3.6 multiply_reduce_fusion.4
  233.2 3.6 multiply_reduce_fusion.5
  236.9 1.7 copy.66
  238.6 3.6 multiply_reduce_fusion.6
  242.3 6.8 %fusion.12 = (f32[2,12,128]{2,1,0:T(8,128)S(1)}, f32[2,12,128]{2,1,0:T(8,128)S(1)}) fusion(f32[2,12,128,512]{3,2,1,0:T(8,128)} %get-tuple-element.68, f32[2,12,128]{2,1,0:T(8,128)S(1)} %get-tuple-element.15, f32[2,12,128]{2,1,0:T(8,128)S(1)} %get-tuple-element.14, f32[2,12,128,512]{3,2,1,0:T(8,128)} %get-tuple-element.66), kind=kLoop, calls=%fused_computation.34 | loop fusion | flops 9431040 | bytes 12632064 | tf_op jit(solution)/shard_map/reduce_sum | solution.py:43
  249.3 4.7 fusion.8
  254.0 8.6 %fusion.403 = (bf16[2,512,768]{2,1,0:T(8,128)(2,1)}, bf16[2,512,768]{2,1,0:T(8,128)(2,1)}, bf16[2,512,768]{2,1,0:T(8,128)(2,1)S(1)}, bf16[2,512,768]{2,1,0:T(8,1...) fusion(bf16[2,4096,768]{2,1,0:T(8,128)(2,1)} %all-gather.8.clon, ...), kind=kLoop, calls=%fused_computation.478 | loop fusion | bytes 25165824 | tf_op jit(solution)/shard_map/slice | solution.py:132
  262.6 2.7 copy.65
  265.3 2.7 copy.68
  268.0 2.6 copy.71
  270.6 2.6 copy.74
  275.6 1.7 copy.83
  277.3 2.6 copy.86
  280.0 6.3 %fusion.4 = (f32[2,12,128]{2,1,0:T(8,128)S(1)}, f32[2,12,128]{2,1,0:T(8,128)S(1)}) fusion(f32[2,12,128,512]{3,2,1,0:T(8,128)} %get-tuple-element.76, f32[2,12,128]{2,1,0:T(8,128)S(1)} %get-tuple-element.19, f32[2,12,128]{2,1,0:T(8,128)S(1)} %get-tuple-element.18, f32[2,12,128,512]{3,2,1,0:T(8,128)} %get-tuple-element.74), kind=kLoop, calls=%fused_computation.26 | loop fusion | flops 9431040 | bytes 12632064 | tf_op jit(solution)/shard_map/reduce_sum | solution.py:43
  286.6 5.0 %fusion = (f32[2,12,128]{2,1,0:T(8,128)S(1)}, f32[2,12,128]{2,1,0:T(8,128)S(1)}) fusion(f32[2,12,128,512]{3,2,1,0:T(8,128)S(1)} %bitcast.416, f32[2,12,128]{2,1,0:T(8,128)S(1)} %get-tuple-element.56, f32[2,12,128]{2,1,0:T(8,128)S(1)} %get-tuple-element.20, f32[2,12,128,512]{3,2,1,0:T(8,128)} %get-tuple-element.78), kind=kLoop, calls=%fused_computation.22 | loop fusion | flops 9431040 | bytes 12632064 | tf_op jit(solution)/shard_map/reduce_sum | solution.py:43
  291.7 1.9 fusion.126
  293.6 1.9 fusion.129
  295.6 1.9 fusion.132
  297.7 1.8 fusion.135
  299.9 1.8 fusion.138
  301.8 1.9 fusion.141
  303.7 1.9 fusion.144
  306.4 2.1 fusion.178
  309.8 50.9 %all-gather.10.cloned.1.call-done = bf16[768,3072]{1,0:T(8,128)(2,1)} async-done(((bf16[768,768]{1,0:T(8,128)(2,1)}), bf16[768,3072]{1,0:T(8,128)(2,1)}) %all-gather.10.cloned.1.call-update) | async-done | bytes 4718608 | tf_op jit(solution)/shard_map/all_gather | solution.py:148
  360.7 12.7 %fusion.152 = bf16[256,768]{1,0:T(8,128)(2,1)S(1)} fusion(f32[256,768]{1,0:T(8,128)S(1)} %get-tuple-element.82, bf16[3072,768]{1,0:T(8,128)(2,1)} %all-gather.12.cloned.1.call-done, bf16[768,3072]{1,0:T(8,128)(2,1)} %all-gather.10.cloned.1.call-done, f32[256]{0:T(256)S(1)} %add_rsqrt_fusion, f32[256]{0:T(256)S(1)} %broadcast_multiply_fusion), kind=kOutput, calls=%fused_computation.136 | convolution fusion | flops 2468020224 | bytes 10618880 | tf_op jit(solution)/shard_map/dot_general | solution.py:153
  373.4 8.8 %gather_fusion.3 = bf16[1024,768]{1,0:T(8,128)(2,1)S(1)} fusion(bf16[2,128,768]{2,1,0:T(8,128)(2,1)S(1)} %bitcast.403, s32[1024]{0:T(1024)S(1)} %reshape.740), kind=kCustom, calls=%fused_computation.3 | custom fusion | bytes 3153920 | tf_op jit(solution)/shard_map/gather | solution.py:165
  383.7 7.6 %all-to-all-start.1 = ((bf16[32,2,16,768]{3,2,1,0:T(8,128)(2,1)}), bf16[32,2,16,768]{3,2,1,0:T(8,128)(2,1)S(1)}, u32[]{:S(2)}, u32[]{:S(2)}) async-start(bf16[32,2,16,768]{3,2,1,0:T(8,128)(2,1)} %broadcast_select_fusion.1), calls=%async_computation.1 | async-start | bytes 3145728 | tf_op jit(solution)/shard_map/all_to_all | solution.py:167
  391.4 21.3 %all-to-all-done.1 = bf16[32,2,16,768]{3,2,1,0:T(8,128)(2,1)S(1)} async-done(((bf16[32,2,16,768]{3,2,1,0:T(8,128)(2,1)}), bf16[32,2,16,768]{3,2,1,0:T(8,128)(2,1)S(1)}, u32[]{:S(2)}, u32[]{:S(2)}) %all-to-all-start.1) | async-done | bytes 1572896 | tf_op jit(solution)/shard_map/all_to_all | solution.py:167
  412.7 9.8 %gather_fusion.4 = bf16[1024,768]{1,0:T(8,128)(2,1)S(1)} fusion(bf16[32,2,16,768]{3,2,1,0:T(8,128)(2,1)S(1)} %all-to-all-done.1, s32[1024]{0:T(1024)S(1)} %bitcast.406), kind=kCustom, calls=%fused_computation.4 | custom fusion | bytes 3158016 | tf_op jit(solution)/shard_map/gather | solution.py:170
  422.6 1.8 fusion.99
  424.4 1.9 collective-permute-start.1
  426.3 2.4 collective-permute-start
  429.1 2.5 collective-permute-done
  431.6 2.4 collective-permute-start.2
  436.0 3.9 collective-permute-done.3
  442.6 2.4 fusion.158
  445.0 1.9 collective-permute-start.5
  447.0 2.4 collective-permute-start.4
  449.7 2.5 collective-permute-done.4
  452.3 3.3 collective-permute-start.6
  457.5 3.9 collective-permute-done.7
  464.4 3.3 convolution_convert_fusion.1
  (189 shorter events, 49.7 us)
Async XLA Ops:
  6.5 114.1 %copy-start = (bf16[768,2304]{1,0:T(8,128)(2,1)S(1)}, bf16[768,2304]{1,0:T(8,128)(2,1)}, u32[]{:S(2)}) copy-start(bf16[768,2304]{1,0:T(8,128)(2,1)} %param.13) | copy-start | bytes 10616836
  9.6 2.2 copy-start.23
  28.9 0.7 copy-start.14
  30.9 9.7 %copy-start.2 = (s32[32,2]{1,0:T(8,128)}, s32[32,2]{1,0:T(8,128)S(1)}, u32[]{:S(2)}) copy-start(s32[32,2]{1,0:T(8,128)S(1)} %get-tuple-element.6) | copy-start | bytes 772
  30.9 0.5 copy-start.20
  83.1 12.8 %copy-start.3 = (s32[32,2]{1,0:T(8,128)S(1)}, s32[32,2]{1,0:T(8,128)}, u32[]{:S(2)}) copy-start(s32[32,2]{1,0:T(8,128)} %copy-done.2) | copy-start | bytes 772
  85.9 28.1 %all-to-all-start = ((bf16[32,2,16,768]{3,2,1,0:T(8,128)(2,1)}), bf16[32,2,16,768]{3,2,1,0:T(8,128)(2,1)}, u32[]{:S(2)}, u32[]{:S(2)}) async-start(bf16[32,2,16,768]{3,2,1,0:T(8,128)(2,1)} %broadcast_select_fusion), calls=%async_computation | async-start | bytes 3145728 | tf_op jit(solution)/shard_map/all_to_all | solution.py:108
  92.5 95.2 %all-gather.6.cloned.1.call-start = ((), (), s32[]{:S(2)}) async-start(), calls=%async_computation.2 | async-start | bytes 12976128 | tf_op jit(solution)/shard_map/all_gather | solution.py:126
  93.9 2.0 copy-start.22
  94.7 0.6 copy-start.19
  122.7 3.1 copy-start.16
  123.7 130.3 %all-gather.8.cloned.1.call-start = ((), (), s32[]{:S(2)}) async-start(), calls=%async_computation.3 | async-start | bytes 12976128 | tf_op jit(solution)/shard_map/all_gather | solution.py:127
  124.5 185.3 %all-gather.12.cloned.1.call-start = ((), (), s32[]{:S(2)}) async-start(), calls=%async_computation.5 | async-start | bytes 5898240 | tf_op jit(solution)/shard_map/all_gather | solution.py:155
  125.2 235.5 %all-gather.10.cloned.1.call-start = ((), (), s32[]{:S(2)}) async-start(), calls=%async_computation.4 | async-start | bytes 5898240 | tf_op jit(solution)/shard_map/all_gather | solution.py:148
  200.9 5.3 %copy-start.10 = (bf16[2,512,768]{1,2,0:T(8,128)(2,1)S(1)}, bf16[2,512,768]{1,2,0:T(8,128)(2,1)}, u32[]{:S(2)}) copy-start(bf16[2,512,768]{1,2,0:T(8,128)(2,1)} %copy.84) | copy-start | bytes 4718596
  242.3 6.8 %slice-start.2 = ((s8[6291456]{0:T(1024)(128)(4,1)}), s8[4194304]{0:T(1024)(128)(4,1)S(1)}, s32[]{:S(2)}) async-start(s8[6291456]{0:T(1024)(128)(4,1)} %bitcast.409), calls=%async_computation.8 | async-start | bytes 8388608
  242.3 7.0 %slice-start.3 = ((s8[6291456]{0:T(1024)(128)(4,1)}), s8[2097152]{0:T(1024)(128)(4,1)S(1)}, s32[]{:S(2)}) async-start(s8[6291456]{0:T(1024)(128)(4,1)} %bitcast.409), calls=%async_computation.9 | async-start | bytes 4194304
  279.9 6.3 %slice-start.8 = ((s8[6291456]{0:T(1024)(128)(4,1)}), s8[4194304]{0:T(1024)(128)(4,1)S(1)}, s32[]{:S(2)}) async-start(s8[6291456]{0:T(1024)(128)(4,1)} %bitcast.415), calls=%async_computation.14 | async-start | bytes 8388608
  279.9 6.7 %slice-start.9 = ((s8[6291456]{0:T(1024)(128)(4,1)}), s8[2097152]{0:T(1024)(128)(4,1)S(1)}, s32[]{:S(2)}) async-start(s8[6291456]{0:T(1024)(128)(4,1)} %bitcast.415), calls=%async_computation.15 | async-start | bytes 4194304
  280.0 13.6 %slice-start.14 = ((s8[6291456]{0:T(1024)(128)(4,1)}), s8[4194304]{0:T(1024)(128)(4,1)S(1)}, s32[]{:S(2)}) async-start(s8[6291456]{0:T(1024)(128)(4,1)} %bitcast.421), calls=%async_computation.20 | async-start | bytes 8388608
  286.6 5.0 %copy-start.9 = (bf16[2,512,768]{1,2,0:T(8,128)(2,1)S(1)}, bf16[2,512,768]{1,2,0:T(8,128)(2,1)}, u32[]{:S(2)}) copy-start(bf16[2,512,768]{1,2,0:T(8,128)(2,1)} %copy.65) | copy-start | bytes 4718596
  286.6 7.0 %slice-start.15 = ((s8[6291456]{0:T(1024)(128)(4,1)}), s8[2097152]{0:T(1024)(128)(4,1)S(1)}, s32[]{:S(2)}) async-start(s8[6291456]{0:T(1024)(128)(4,1)} %bitcast.421), calls=%async_computation.21 | async-start | bytes 4194304
  286.6 8.9 %slice-start.12 = ((s8[6291456]{0:T(1024)(128)(4,1)}), s8[4194304]{0:T(1024)(128)(4,1)S(1)}, s32[]{:S(2)}) async-start(s8[6291456]{0:T(1024)(128)(4,1)} %bitcast.419), calls=%async_computation.18 | async-start | bytes 8388608
  291.7 1.9 copy-start.7
  291.7 3.9 slice-start.13
  291.7 5.8 %slice-start.10 = ((s8[6291456]{0:T(1024)(128)(4,1)}), s8[4194304]{0:T(1024)(128)(4,1)S(1)}, s32[]{:S(2)}) async-start(s8[6291456]{0:T(1024)(128)(4,1)} %bitcast.417), calls=%async_computation.16 | async-start | bytes 8388608
  293.6 1.9 copy-start.6
  293.6 3.8 slice-start.11
  293.6 5.9 %slice-start.6 = ((s8[6291456]{0:T(1024)(128)(4,1)}), s8[4194304]{0:T(1024)(128)(4,1)S(1)}, s32[]{:S(2)}) async-start(s8[6291456]{0:T(1024)(128)(4,1)} %bitcast.413), calls=%async_computation.12 | async-start | bytes 8388608
  295.5 2.2 copy-start.5
  295.6 4.0 slice-start.7
  295.6 6.1 %slice-start.4 = ((s8[6291456]{0:T(1024)(128)(4,1)}), s8[4194304]{0:T(1024)(128)(4,1)S(1)}, s32[]{:S(2)}) async-start(s8[6291456]{0:T(1024)(128)(4,1)} %bitcast.411), calls=%async_computation.10 | async-start | bytes 8388608
  297.7 2.2 copy-start.4
  297.7 4.0 slice-start.5
  299.9 3.8 slice-start
  301.7 1.9 slice-start.1
  301.7 3.8 slice-start.16
  303.7 2.3 slice-start.17
  303.7 2.7 copy-start.12
  306.4 2.5 copy-start.8
  306.4 2.5 copy-start.13
  373.4 8.8 %copy-start.17 = (pred[32,2,16]{2,1,0:T(4,128)(4,1)S(1)}, pred[32,2,16]{2,1,0:T(4,128)(4,1)}, u32[]{:S(2)}) copy-start(pred[32,2,16]{2,1,0:T(4,128)(4,1)} %get-tuple-element.61) | copy-start | bytes 3076
  382.2 9.0 %copy-start.18 = (s32[2,4,128]{2,1,0:T(4,128)S(1)}, s32[2,4,128]{2,1,0:T(4,128)}, u32[]{:S(2)}) copy-start(s32[2,4,128]{2,1,0:T(4,128)} %get-tuple-element.57) | copy-start | bytes 12292
  382.3 9.0 %copy-start.21 = (s32[2]{0:T(128)S(1)}, s32[2]{0:T(128)}, u32[]{:S(2)}) copy-start(s32[2]{0:T(128)} %copy-done.20) | copy-start | bytes 28
  382.3 9.1 %copy-start.15 = (s32[2,16,32]{2,1,0:T(8,128)S(1)}, s32[2,16,32]{2,1,0:T(8,128)}, u32[]{:S(2)}) copy-start(s32[2,16,32]{2,1,0:T(8,128)} %param.11) | copy-start | bytes 12292
  383.7 29.1 %all-to-all-start.1 = ((bf16[32,2,16,768]{3,2,1,0:T(8,128)(2,1)}), bf16[32,2,16,768]{3,2,1,0:T(8,128)(2,1)S(1)}, u32[]{:S(2)}, u32[]{:S(2)}) async-start(bf16[32,2,16,768]{3,2,1,0:T(8,128)(2,1)} %broadcast_select_fusion.1), calls=%async_computation.1 | async-start | bytes 3145728 | tf_op jit(solution)/shard_map/all_to_all | solution.py:167
  412.7 9.9 %copy-start.25 = (bf16[768]{0:T(1024)(128)(2,1)S(1)}, bf16[768]{0:T(1024)(128)(2,1)}, u32[]{:S(2)}) copy-start(bf16[768]{0:T(1024)(128)(2,1)} %param.12) | copy-start | bytes 4612
  422.6 6.2 %copy-start.11 = (bf16[2,9,256,256]{3,2,1,0:T(8,128)(2,1)S(1)}, bf16[2,9,256,256]{3,2,1,0:T(8,128)(2,1)}, u32[]{:S(2)}) copy-start(bf16[2,9,256,256]{3,2,1,0:T(8,128)(2,1)} %param.18) | copy-start | bytes 7077892
  424.4 4.7 collective-permute-start.1
  426.3 5.2 %collective-permute-start = (bf16[2,1,32,256]{3,2,1,0:T(8,128)(2,1)S(1)}, bf16[2,1,32,256]{3,2,1,0:T(8,128)(2,1)S(1)}, u32[]{:S(2)}, u32[]{:S(2)}) collective-permute-start(bf16[2,1,32,256]{3,2,1,0:T(8,128)(2,1)S(1)} %get-tuple-element.52), channel_id=1, source_target_pairs={{0,4},{4,8},{8,12},{12,16},{16,20},{20,24},{24,28},{1,5},{5,9},{9,... | collective-permute-start | bytes 98312 | tf_op jit(solution)/shard_map/ppermute | solution.py:20
  431.6 4.3 collective-permute-start.2
  434.0 5.9 %collective-permute-start.3 = (bf16[2,18,1,256]{3,2,1,0:T(2,128)(2,1)S(1)}, bf16[2,18,1,256]{3,2,1,0:T(2,128)(2,1)S(1)}, u32[]{:S(2)}, u32[]{:S(2)}) collective-permute-start(bf16[2,18,1,256]{3,2,1,0:T(2,128)(2,1)S(1)} %get-tuple-element.49), channel_id=1, source_target_pairs={{1,0},{2,1},{3,2},{5,4},{6,5},{7,6},{9,8},{10,9},{11,10},{13,12},{... | collective-permute-start | bytes 55304 | tf_op jit(solution)/shard_map/ppermute | solution.py:22
  445.0 4.6 collective-permute-start.5
  447.0 5.2 %collective-permute-start.4 = (bf16[2,1,32,256]{3,2,1,0:T(8,128)(2,1)S(1)}, bf16[2,1,32,256]{3,2,1,0:T(8,128)(2,1)S(1)}, u32[]{:S(2)}, u32[]{:S(2)}) collective-permute-start(bf16[2,1,32,256]{3,2,1,0:T(8,128)(2,1)S(1)} %get-tuple-element.50), channel_id=1, source_target_pairs={{0,4},{4,8},{8,12},{12,16},{16,20},{20,24},{24,28},{1,5},{5,9},{9,... | collective-permute-start | bytes 98312 | tf_op jit(solution)/shard_map/ppermute | solution.py:20
  452.3 5.2 %collective-permute-start.6 = (bf16[2,18,1,256]{3,2,1,0:T(2,128)(2,1)S(1)}, bf16[2,18,1,256]{3,2,1,0:T(2,128)(2,1)S(1)}, u32[]{:S(2)}, u32[]{:S(2)}) collective-permute-start(bf16[2,18,1,256]{3,2,1,0:T(2,128)(2,1)S(1)} %get-tuple-element.44), channel_id=1, source_target_pairs={{0,1},{1,2},{2,3},{4,5},{5,6},{6,7},{8,9},{9,10},{10,11},{12,13},{... | collective-permute-start | bytes 55304 | tf_op jit(solution)/shard_map/ppermute | solution.py:20
  455.6 5.9 %collective-permute-start.7 = (bf16[2,18,1,256]{3,2,1,0:T(2,128)(2,1)S(1)}, bf16[2,18,1,256]{3,2,1,0:T(2,128)(2,1)S(1)}, u32[]{:S(2)}, u32[]{:S(2)}) collective-permute-start(bf16[2,18,1,256]{3,2,1,0:T(2,128)(2,1)S(1)} %get-tuple-element.45), channel_id=1, source_target_pairs={{1,0},{2,1},{3,2},{5,4},{6,5},{7,6},{9,8},{10,9},{11,10},{13,12},{... | collective-permute-start | bytes 55304 | tf_op jit(solution)/shard_map/ppermute | solution.py:22
  463.5 0.8 copy-start.24
  464.4 3.3 copy-start.1
Sparse Core Ops, SparseCore 0:
  123.9 63.7 all-gather.5
  190.0 62.3 all-gather.7
  254.1 52.0 all-gather.11
  307.7 52.9 all-gather.9
where the time goes:
time: 483 us; the launch traced here: 474 us
  waiting for transfers between devices  163 us (34%)
  local copies, waits for them, and re-layouts  128 us (27%)
  matrix products  72.7 us (15%)
  other arithmetic  48 us (10%)
  starting transfers between devices  31.4 us (7%)
  blocking collectives  16.4 us (3%)
  between operations  15 us (3%)
    all_gather x1, waiting for transfers between devices, shards(): keys_piece = lax.all_gather(keys_local, ('row', 'col'), axis=1, tiled=True)  61.5 us
    all_gather x1, waiting for transfers between devices, shards(): lax.all_gather(up_weight, 'dp', axis=1, tiled=True)  50.9 us
    dot_general x8, matrix products, attend(): jnp.einsum('sqhd,skhd->shqk', query, keys, preferred_element_type=jnp.flo...  30.9 us
    gather x1, local copies, waits for them, and re-layouts, shards(): flat_tokens[sample_ids, source_pos]  29.2 us
    slice x9, local copies, waits for them, and re-layouts, shards(): values_piece[:, lower:upper].reshape(samples, upper - lower, HEADS, HD)  25.9 us
    slice x9, local copies, waits for them, and re-layouts, shards(): keys_piece[:, lower:upper].reshape(samples, upper - lower, HEADS, HD)  23.6 us
    reduce_sum x4, other arithmetic, attend(): run_sum = run_sum * shrink + jnp.sum(expo, -1)  22.7 us
    all_to_all x1, waiting for transfers between devices, shards(): lax.all_to_all(returning, ('row', 'col'), split_axis=0, concat_axis=0, ti...  21.3 us
  transfers between devices with their start and end apart: 14, of which 8 were waited for; matrix products, arithmetic and copies ran while one was open for 27% of the time, Pallas kernels for 0%

commit v1 on v0

--- a/solution.py
+++ b/solution.py
@@ -123,7 +123,10 @@
     keys_local = qkv[:, width : 2 * width].reshape(samples, kept_dev, width)
     values_local = qkv[:, 2 * width :].reshape(samples, kept_dev, width)
     carry = init_carry
-    keys_piece = lax.all_gather(keys_local, ("row", "col"), axis=1, tiled=True)
+    peers_2 = lax.axis_size(("row", "col"))
+    parts = jnp.stack([keys_local for _ in range(peers_2)])
+    parts = lax.all_to_all(parts, ("row", "col"), split_axis=0, concat_axis=0)
+    keys_piece = jnp.concatenate(parts, axis=1)
     values_piece = lax.all_gather(values_local, ("row", "col"), axis=1, tiled=True)
     count = keys_piece.shape[1]
     for lower in range(0, count, BLOCK):

time: 483 us -> 603 us (1.25)
  the two profiles are of different devices: /device:TPU:2 before, /device:TPU:18 now
where the time goes in v1:
time: 603 us; the launch traced here: 592 us
  waiting for transfers between devices  232 us (38%)
  local copies, waits for them, and re-layouts  154 us (26%)
  matrix products  77.4 us (13%)
  starting transfers between devices  52.4 us (9%)
  other arithmetic  44.9 us (7%)
  blocking collectives  16.4 us (3%)
  between operations  15.1 us (3%)
    all_to_all x1, waiting for transfers between devices, shards(): parts = lax.all_to_all(parts, ('row', 'col'), split_axis=0, concat_axis=0)  182 us
    gather x1, local copies, waits for them, and re-layouts, shards(): flat_tokens[sample_ids, source_pos]  32.1 us
    dot_general x8, matrix products, attend(): jnp.einsum('sqhd,skhd->shqk', query, keys, preferred_element_type=jnp.flo...  28.5 us
    slice x9, local copies, waits for them, and re-layouts, shards(): values_piece[:, lower:upper].reshape(samples, upper - lower, HEADS, HD)  25.7 us
    slice x9, local copies, waits for them, and re-layouts, shards(): keys_piece[:, lower:upper].reshape(samples, upper - lower, HEADS, HD)  23.8 us
    all_to_all x1, starting transfers between devices, shards(): lax.all_to_all(returning, ('row', 'col'), split_axis=0, concat_axis=0, ti...  23.5 us
    dot_general x8, matrix products, attend(): jnp.einsum('shqk,skhd->sqhd', expo.astype(jnp.bfloat16), values, preferre...  22.2 us
    all_to_all x1, waiting for transfers between devices, shards(): lax.all_to_all(returning, ('row', 'col'), split_axis=0, concat_axis=0, ti...  21.3 us
  transfers between devices with their start and end apart: 14, of which 7 were waited for; matrix products, arithmetic and copies ran while one was open for 26% of the time, Pallas kernels for 0%

profile of v1, /device:TPU:18, one launch (start us, length us, event | category | flops | bytes accessed | tf_op | source)
XLA Modules:
  0.0 592.4 jit_solution(12743487238965291697)
XLA Ops:
  11.7 16.4 %all-reduce = s32[64]{0:T(128)} all-reduce(s32[64]{0:T(128)S(1)} %dynamic-update-slice), channel_id=2, replica_groups=mesh['dp'=4,'row'=8,'col'=4] {'row','col'}, use_global_device_ids=true, to_apply=%add | all-reduce | flops 64 | bytes 512
  34.5 1.9 reduce-window.6
  41.7 9.1 %gather_fusion = s32[1024]{0:T(1024)S(1)} fusion(s32[2,512]{1,0:T(2,128)S(1)} %convert_reduce_fusion, s32[1024]{0:T(1024)S(1)} %reshape.728), kind=kCustom, calls=%fused_computation | custom fusion | bytes 16384 | tf_op jit(solution)/shard_map/gather | solution.py:104
  53.8 32.1 %gather_fusion.1 = bf16[1024,768]{1,0:T(8,128)(2,1)} fusion(bf16[2,512,768]{2,1,0:T(8,128)(2,1)} %bitcast.407, s32[1024]{0:T(1024)S(1)} %reshape.734), kind=kCustom, calls=%fused_computation.1 | custom fusion | bytes 3153920 | tf_op jit(solution)/shard_map/gather | solution.py:106
  85.9 2.8 broadcast_select_fusion
  88.7 5.4 all-to-all-start
  97.5 2.7 gather_fusion.5
  101.0 14.8 %all-to-all-done = bf16[32,2,16,768]{3,2,1,0:T(8,128)(2,1)} async-done(((bf16[32,2,16,768]{3,2,1,0:T(8,128)(2,1)}), bf16[32,2,16,768]{3,2,1,0:T(8,128)(2,1)}, u32[]{:S(2)}, u32[]{:S(2)}) %all-to-all-start) | async-done | bytes 1572896 | tf_op jit(solution)/shard_map/all_to_all | solution.py:108
  115.7 4.2 gather_fusion.2
  122.3 2.1 convolution_convert_fusion
  125.5 7.6 %stack.3 = bf16[32,2,128,768]{2,3,1,0:T(8,128)(2,1)} broadcast(bf16[2,128,768]{1,2,0:T(8,128)(2,1)S(1)} %copy.96), dimensions={1,2,3} | broadcast | bytes 12976128 | tf_op jit(solution)/shard_map/stack | solution.py:127
  133.1 6.2 %all-to-all-start.1 = ((bf16[32,2,128,768]{2,3,1,0:T(8,128)(2,1)}), bf16[32,2,128,768]{2,3,1,0:T(8,128)(2,1)}, u32[]{:S(2)}, u32[]{:S(2)}) async-start(bf16[32,2,128,768]{2,3,1,0:T(8,128)(2,1)} %stack.3), calls=%async_computation.1 | async-start | bytes 25165824 | tf_op jit(solution)/shard_map/all_to_all | solution.py:128
  141.2 181.9 %all-to-all-done.1 = bf16[32,2,128,768]{2,3,1,0:T(8,128)(2,1)} async-done(((bf16[32,2,128,768]{2,3,1,0:T(8,128)(2,1)}), bf16[32,2,128,768]{2,3,1,0:T(8,128)(2,1)}, u32[]{:S(2)}, u32[]{:S(2)}) %all-to-all-start.1) | async-done | bytes 12582944 | tf_op jit(solution)/shard_map/all_to_all | solution.py:128
  323.1 16.9 %copy.97 = bf16[32,2,128,768]{3,2,0,1:T(8,128)(2,1)} copy(bf16[32,2,128,768]{2,3,1,0:T(8,128)(2,1)} %all-to-all-done.1) | data formatting | bytes 25165824 | tf_op jit(solution)/shard_map/all_to_all | solution.py:128
  340.0 9.2 %fusion.404 = (bf16[2,512,768]{2,1,0:T(8,128)(2,1)}, bf16[2,512,768]{2,1,0:T(8,128)(2,1)S(1)}, bf16[2,512,768]{2,1,0:T(8,128)(2,1)}, bf16[2,512,768]{2,1,0:T(8,1...) fusion(bf16[2,4096,768]{2,1,0:T(8,128)(2,1)} %bitcast.426), kind=kLoop, calls=%fused_computation.479 | loop fusion | bytes 25165824 | tf_op jit(solution)/shard_map/slice | solution.py:134
  349.2 2.6 copy.98
  353.4 5.3 multiply_reduce_fusion.7
  358.7 3.6 multiply_reduce_fusion
  362.3 1.7 copy.116
  364.1 3.7 multiply_reduce_fusion.1
  367.7 1.7 copy.113
  369.5 3.7 multiply_reduce_fusion.2
  373.2 1.7 copy.110
  374.9 3.7 multiply_reduce_fusion.3
  380.3 3.8 multiply_reduce_fusion.4
  384.1 1.8 copy.104
  385.9 3.6 multiply_reduce_fusion.5
  389.5 1.7 copy.101
  392.4 8.9 %fusion.12 = (f32[2,12,128]{2,1,0:T(8,128)S(1)}, f32[2,12,128]{2,1,0:T(8,128)S(1)}) fusion(f32[2,12,128,512]{3,2,1,0:T(8,128)} %get-tuple-element.68, f32[2,12,128]{2,1,0:T(8,128)S(1)} %get-tuple-element.15, f32[2,12,128]{2,1,0:T(8,128)S(1)} %get-tuple-element.14, f32[2,12,128,512]{3,2,1,0:T(8,128)} %get-tuple-element.66), kind=kLoop, calls=%fused_computation.34 | loop fusion | flops 9431040 | bytes 12632064 | tf_op jit(solution)/shard_map/reduce_sum | solution.py:43
  401.6 4.9 fusion.8
  406.6 2.9 fusion.4
  409.6 2.9 fusion
  412.6 8.6 %fusion.403 = (bf16[2,512,768]{2,1,0:T(8,128)(2,1)}, bf16[2,512,768]{2,1,0:T(8,128)(2,1)}, bf16[2,512,768]{2,1,0:T(8,128)(2,1)S(1)}, bf16[2,512,768]{2,1,0:T(8,1...) fusion(bf16[2,4096,768]{2,1,0:T(8,128)(2,1)} %all-gather.5.clon, ...), kind=kLoop, calls=%fused_computation.478 | loop fusion | bytes 25165824 | tf_op jit(solution)/shard_map/slice | solution.py:135
  421.2 2.6 copy.100
  423.8 2.6 copy.103
  426.4 2.7 copy.106
  429.0 2.6 copy.109
  433.9 1.7 copy.118
  435.7 2.6 copy.121
  438.3 4.9 fusion.126
  443.2 3.9 fusion.129
  447.1 3.9 fusion.132
  451.1 1.9 fusion.135
  453.0 1.9 fusion.138
  455.0 1.9 fusion.141
  456.9 2.3 fusion.144
  462.6 12.8 %fusion.152 = bf16[256,768]{1,0:T(8,128)(2,1)S(1)} fusion(f32[256,768]{1,0:T(8,128)S(1)} %get-tuple-element.82, bf16[3072,768]{1,0:T(8,128)(2,1)} %all-gather.9.cloned.1.call-done, bf16[768,3072]{1,0:T(8,128)(2,1)} %all-gather.7.cloned.1.call-done, f32[256]{0:T(256)S(1)} %add_rsqrt_fusion, f32[256]{0:T(256)S(1)} %broadcast_multiply_fusion), kind=kOutput, calls=%fused_computation.136 | convolution fusion | flops 2468020224 | bytes 10618880 | tf_op jit(solution)/shard_map/dot_general | solution.py:156
  475.4 9.0 %gather_fusion.3 = bf16[1024,768]{1,0:T(8,128)(2,1)S(1)} fusion(bf16[2,128,768]{2,1,0:T(8,128)(2,1)S(1)} %bitcast.406, s32[1024]{0:T(1024)S(1)} %reshape.746), kind=kCustom, calls=%fused_computation.3 | custom fusion | bytes 3153920 | tf_op jit(solution)/shard_map/gather | solution.py:168
  485.8 23.5 %all-to-all-start.2 = ((bf16[32,2,16,768]{3,2,1,0:T(8,128)(2,1)}), bf16[32,2,16,768]{3,2,1,0:T(8,128)(2,1)S(1)}, u32[]{:S(2)}, u32[]{:S(2)}) async-start(bf16[32,2,16,768]{3,2,1,0:T(8,128)(2,1)} %broadcast_select_fusion.1), calls=%async_computation.2 | async-start | bytes 3145728 | tf_op jit(solution)/shard_map/all_to_all | solution.py:170
  509.5 21.3 %all-to-all-done.2 = bf16[32,2,16,768]{3,2,1,0:T(8,128)(2,1)S(1)} async-done(((bf16[32,2,16,768]{3,2,1,0:T(8,128)(2,1)}), bf16[32,2,16,768]{3,2,1,0:T(8,128)(2,1)S(1)}, u32[]{:S(2)}, u32[]{:S(2)}) %all-to-all-start.2) | async-done | bytes 1572896 | tf_op jit(solution)/shard_map/all_to_all | solution.py:170
  530.8 9.8 %gather_fusion.4 = bf16[1024,768]{1,0:T(8,128)(2,1)S(1)} fusion(bf16[32,2,16,768]{3,2,1,0:T(8,128)(2,1)S(1)} %all-to-all-done.2, s32[1024]{0:T(1024)S(1)} %bitcast.409), kind=kCustom, calls=%fused_computation.4 | custom fusion | bytes 3158016 | tf_op jit(solution)/shard_map/gather | solution.py:173
  540.7 1.8 fusion.99
  542.5 1.9 collective-permute-start.1
  544.4 2.4 collective-permute-start
  547.1 2.5 collective-permute-done
  549.7 2.4 collective-permute-start.2
  554.0 3.9 collective-permute-done.3
  560.7 2.4 fusion.158
  563.1 1.9 collective-permute-start.5
  565.1 2.4 collective-permute-start.4
  567.8 2.5 collective-permute-done.4
  570.4 3.3 collective-permute-start.6
  575.6 3.9 collective-permute-done.7
  582.5 3.3 convolution_convert_fusion.1
  (191 shorter events, 50.7 us)
Async XLA Ops:
  6.5 115.8 %copy-start = (bf16[768,2304]{1,0:T(8,128)(2,1)S(1)}, bf16[768,2304]{1,0:T(8,128)(2,1)}, u32[]{:S(2)}) copy-start(bf16[768,2304]{1,0:T(8,128)(2,1)} %param.13) | copy-start | bytes 10616836
  9.5 2.2 copy-start.23
  28.9 0.7 copy-start.14
  30.9 9.7 %copy-start.2 = (s32[32,2]{1,0:T(8,128)}, s32[32,2]{1,0:T(8,128)S(1)}, u32[]{:S(2)}) copy-start(s32[32,2]{1,0:T(8,128)S(1)} %get-tuple-element.6) | copy-start | bytes 772
  30.9 0.5 copy-start.20
  85.9 11.6 %copy-start.3 = (s32[32,2]{1,0:T(8,128)S(1)}, s32[32,2]{1,0:T(8,128)}, u32[]{:S(2)}) copy-start(s32[32,2]{1,0:T(8,128)} %copy-done.2) | copy-start | bytes 772
  88.7 27.1 %all-to-all-start = ((bf16[32,2,16,768]{3,2,1,0:T(8,128)(2,1)}), bf16[32,2,16,768]{3,2,1,0:T(8,128)(2,1)}, u32[]{:S(2)}, u32[]{:S(2)}) async-start(bf16[32,2,16,768]{3,2,1,0:T(8,128)(2,1)} %broadcast_select_fusion), calls=%async_computation | async-start | bytes 3145728 | tf_op jit(solution)/shard_map/all_to_all | solution.py:108
  94.1 318.5 %all-gather.5.cloned.1.call-start = ((), (), s32[]{:S(2)}) async-start(), calls=%async_computation.3 | async-start | bytes 12976128 | tf_op jit(solution)/shard_map/all_gather | solution.py:130
  95.6 2.0 copy-start.22
  96.3 0.6 copy-start.19
  133.1 7.7 %copy-start.16 = (s32[32,2,16,1]{2,1,0,3:T(2,128)S(1)}, s32[32,2,16,1]{2,1,0,3:T(2,128)}, u32[]{:S(2)}) copy-start(s32[32,2,16,1]{2,1,0,3:T(2,128)} %get-tuple-element.63) | copy-start | bytes 12292
  133.1 190.0 %all-to-all-start.1 = ((bf16[32,2,128,768]{2,3,1,0:T(8,128)(2,1)}), bf16[32,2,128,768]{2,3,1,0:T(8,128)(2,1)}, u32[]{:S(2)}, u32[]{:S(2)}) async-start(bf16[32,2,128,768]{2,3,1,0:T(8,128)(2,1)} %stack.3), calls=%async_computation.1 | async-start | bytes 25165824 | tf_op jit(solution)/shard_map/all_to_all | solution.py:128
  139.3 323.3 %all-gather.9.cloned.1.call-start = ((), (), s32[]{:S(2)}) async-start(), calls=%async_computation.5 | async-start | bytes 5898240 | tf_op jit(solution)/shard_map/all_gather | solution.py:158
  140.1 322.5 %all-gather.7.cloned.1.call-start = ((), (), s32[]{:S(2)}) async-start(), calls=%async_computation.4 | async-start | bytes 5898240 | tf_op jit(solution)/shard_map/all_gather | solution.py:151
  353.4 5.3 copy-start.10
  391.2 15.3 %slice-start.14 = ((s8[6291456]{0:T(1024)(128)(4,1)}), s8[4194304]{0:T(1024)(128)(4,1)S(1)}, s32[]{:S(2)}) async-start(s8[6291456]{0:T(1024)(128)(4,1)} %bitcast.424), calls=%async_computation.20 | async-start | bytes 8388608
  392.4 17.2 %copy-start.4 = (f32[2,12,128,512]{3,2,1,0:T(8,128)}, f32[2,12,128,512]{3,2,1,0:T(8,128)S(1)}, u32[]{:S(2)}) copy-start(f32[2,12,128,512]{3,2,1,0:T(8,128)S(1)} %get-tuple-element.78) | copy-start | bytes 18874372
  392.4 8.9 %slice-start.2 = ((s8[6291456]{0:T(1024)(128)(4,1)}), s8[4194304]{0:T(1024)(128)(4,1)S(1)}, s32[]{:S(2)}) async-start(s8[6291456]{0:T(1024)(128)(4,1)} %bitcast.412), calls=%async_computation.8 | async-start | bytes 8388608
  392.4 9.2 %slice-start.3 = ((s8[6291456]{0:T(1024)(128)(4,1)}), s8[2097152]{0:T(1024)(128)(4,1)S(1)}, s32[]{:S(2)}) async-start(s8[6291456]{0:T(1024)(128)(4,1)} %bitcast.412), calls=%async_computation.9 | async-start | bytes 4194304
  392.4 14.1 %slice-start.15 = ((s8[6291456]{0:T(1024)(128)(4,1)}), s8[2097152]{0:T(1024)(128)(4,1)S(1)}, s32[]{:S(2)}) async-start(s8[6291456]{0:T(1024)(128)(4,1)} %bitcast.424), calls=%async_computation.21 | async-start | bytes 4194304
  401.3 5.2 slice-start.10
  401.6 4.9 slice-start.11
  406.5 3.1 slice-start.8
  406.6 3.0 slice-start.9
  438.3 4.9 copy-start.8
  438.3 12.8 %slice-start.12 = ((s8[6291456]{0:T(1024)(128)(4,1)}), s8[4194304]{0:T(1024)(128)(4,1)S(1)}, s32[]{:S(2)}) async-start(s8[6291456]{0:T(1024)(128)(4,1)} %bitcast.422), calls=%async_computation.18 | async-start | bytes 8388608
  443.2 3.9 copy-start.7
  443.2 7.9 %slice-start.13 = ((s8[6291456]{0:T(1024)(128)(4,1)}), s8[2097152]{0:T(1024)(128)(4,1)S(1)}, s32[]{:S(2)}) async-start(s8[6291456]{0:T(1024)(128)(4,1)} %bitcast.422), calls=%async_computation.19 | async-start | bytes 4194304
  443.2 9.8 %slice-start.6 = ((s8[6291456]{0:T(1024)(128)(4,1)}), s8[4194304]{0:T(1024)(128)(4,1)S(1)}, s32[]{:S(2)}) async-start(s8[6291456]{0:T(1024)(128)(4,1)} %bitcast.416), calls=%async_computation.12 | async-start | bytes 8388608
  447.1 4.0 copy-start.6
  447.1 5.9 slice-start.7
  447.1 7.8 %slice-start.4 = ((s8[6291456]{0:T(1024)(128)(4,1)}), s8[4194304]{0:T(1024)(128)(4,1)S(1)}, s32[]{:S(2)}) async-start(s8[6291456]{0:T(1024)(128)(4,1)} %bitcast.414), calls=%async_computation.10 | async-start | bytes 8388608
  451.1 1.9 copy-start.5
  451.1 3.8 slice-start.5
  453.0 3.8 slice-start
  454.9 1.9 slice-start.1
  455.0 4.2 slice-start.16
  456.9 2.3 slice-start.17
  456.9 2.7 copy-start.12
  459.6 2.1 copy-start.9
  459.6 2.1 copy-start.13
  475.4 9.0 %copy-start.17 = (pred[32,2,16]{2,1,0:T(4,128)(4,1)S(1)}, pred[32,2,16]{2,1,0:T(4,128)(4,1)}, u32[]{:S(2)}) copy-start(pred[32,2,16]{2,1,0:T(4,128)(4,1)} %get-tuple-element.61) | copy-start | bytes 3076
  484.4 25.0 %copy-start.18 = (s32[2,4,128]{2,1,0:T(4,128)S(1)}, s32[2,4,128]{2,1,0:T(4,128)}, u32[]{:S(2)}) copy-start(s32[2,4,128]{2,1,0:T(4,128)} %get-tuple-element.57) | copy-start | bytes 12292
  484.4 25.0 %copy-start.21 = (s32[2]{0:T(128)S(1)}, s32[2]{0:T(128)}, u32[]{:S(2)}) copy-start(s32[2]{0:T(128)} %copy-done.20) | copy-start | bytes 28
  484.4 25.1 %copy-start.15 = (s32[2,16,32]{2,1,0:T(8,128)S(1)}, s32[2,16,32]{2,1,0:T(8,128)}, u32[]{:S(2)}) copy-start(s32[2,16,32]{2,1,0:T(8,128)} %param.11) | copy-start | bytes 12292
  485.8 45.0 %all-to-all-start.2 = ((bf16[32,2,16,768]{3,2,1,0:T(8,128)(2,1)}), bf16[32,2,16,768]{3,2,1,0:T(8,128)(2,1)S(1)}, u32[]{:S(2)}, u32[]{:S(2)}) async-start(bf16[32,2,16,768]{3,2,1,0:T(8,128)(2,1)} %broadcast_select_fusion.1), calls=%async_computation.2 | async-start | bytes 3145728 | tf_op jit(solution)/shard_map/all_to_all | solution.py:170
  530.8 9.9 %copy-start.25 = (bf16[768]{0:T(1024)(128)(2,1)S(1)}, bf16[768]{0:T(1024)(128)(2,1)}, u32[]{:S(2)}) copy-start(bf16[768]{0:T(1024)(128)(2,1)} %param.12) | copy-start | bytes 4612
  540.6 6.2 %copy-start.11 = (bf16[2,9,256,256]{3,2,1,0:T(8,128)(2,1)S(1)}, bf16[2,9,256,256]{3,2,1,0:T(8,128)(2,1)}, u32[]{:S(2)}) copy-start(bf16[2,9,256,256]{3,2,1,0:T(8,128)(2,1)} %param.18) | copy-start | bytes 7077892
  542.5 4.7 collective-permute-start.1
  544.4 5.2 collective-permute-start
  549.7 4.3 collective-permute-start.2
  552.1 5.9 collective-permute-start.3
  563.1 4.6 collective-permute-start.5
  565.1 5.2 collective-permute-start.4
  570.4 5.2 collective-permute-start.6
  573.7 5.9 collective-permute-start.7
  581.6 0.8 copy-start.24
  582.4 3.3 copy-start.1
Sparse Core Ops, SparseCore 0:
  125.4 187.7 all-gather.4
  314.8 54.9 all-gather.8
  371.5 52.9 all-gather.6
